TPU v7x, 32 devices: a whole 2x2x4 slice. The times are simulated.
32 devices in a mesh: groups: 2 (over y), dap: 4 (over z), chan: 2 (over x), sub: 2 (over core).
Axes of the slice: x: 2, y: 2, z: 4, core: 2. Of those that a mesh axis runs over, the one named last changes fastest.
Arguments:
- pair_input: bfloat16 [768, 384, 128], P(('groups', 'dap'), ('chan', 'sub')), parts along dimension 0, may hold values from -6 to 6
- first_gain: float32 [128], replicated, may hold values from 0.25 to 1.75
- first_project: bfloat16 [128, 512], replicated, may hold values from -0.5 to 0.5
- first_gate: bfloat16 [128, 128], replicated, may hold values from -0.5 to 0.5
- first_norm: float32 [128], replicated, may hold values from 0.25 to 1.75
- first_final: bfloat16 [128, 128], replicated, may hold values from -0.5 to 0.5
- second_gain: float32 [128], replicated, may hold values from 0.25 to 1.75
- second_project: bfloat16 [128, 512], replicated, may hold values from -0.5 to 0.5
- second_gate: bfloat16 [128, 128], replicated, may hold values from -0.5 to 0.5
- second_norm: float32 [128], replicated, may hold values from 0.25 to 1.75
- second_final: bfloat16 [128, 128], replicated, may hold values from -0.5 to 0.5
Outputs:
- pair_output: bfloat16 [768, 384, 128], P(('groups', 'dap'), ('chan', 'sub')), parts along dimension 0
There are 2 independent parts, one for each index of `groups`. A program takes and returns all parts, laid end to end along the dimension named above; an argument that names none is the same for every part. Nothing has to cross between parts.
All inputs are finite; a program needn't handle non-finite values.
Results may differ from a plain program's by a relative error of at most 0.013.
Values may be sent and summed in bfloat16 or wider, within the bound.
No kernel may reach another device: no remote copies, remote signals or barrier semaphores. Data moves between devices by JAX's collectives and lax.ppermute only.
A program may use at most 64 MiB of HBM per device.

v0:
```python
import jax
import jax.numpy as jnp
from jax import lax
from jax.sharding import PartitionSpec as P

epsilon = 1e-05


def layer_norm(values, norm_gain, reduce_axis):
    average = jnp.mean(values, axis=reduce_axis, keepdims=True)
    centred = values - average
    variance = jnp.mean(centred * centred, axis=reduce_axis, keepdims=True)
    return centred * lax.rsqrt(variance + epsilon) * norm_gain


def project_in(pair_state, norm_gain, project, gate_matrix):
    row_count, col_count, features = pair_state.shape
    flattened = pair_state.reshape(row_count * col_count, features).astype(jnp.float32)
    normed = layer_norm(flattened, norm_gain, 1).astype(jnp.bfloat16)
    projected = jnp.einsum("xc,cd->dx", normed, project, preferred_element_type=jnp.float32)
    left_part = jax.nn.sigmoid(projected[:features]) * projected[features : 2 * features]
    right_part = jax.nn.sigmoid(projected[2 * features : 3 * features]) * projected[3 * features :]
    left_part = left_part.astype(jnp.bfloat16).reshape(features, row_count, col_count)
    right_part = right_part.astype(jnp.bfloat16).reshape(features, row_count, col_count)
    gating = jax.nn.sigmoid(jnp.dot(normed, gate_matrix, preferred_element_type=jnp.float32))
    return (left_part, right_part, gating)


def finish(pair_state, mixture, gating, out_gain, final_matrix):
    features = mixture.shape[0]
    flattened = mixture.reshape(features, -1).astype(jnp.float32)
    normed = layer_norm(flattened, out_gain[:, None], 0).astype(jnp.bfloat16)
    update = jnp.einsum("cx,cd->xd", normed, final_matrix, preferred_element_type=jnp.float32)
    result = pair_state.reshape(-1, features).astype(jnp.float32) + gating * update
    return result.astype(jnp.bfloat16).reshape(pair_state.shape)


def shards(
    pair_input,
    first_gain,
    first_project,
    first_gate,
    first_norm,
    first_final,
    second_gain,
    second_project,
    second_gate,
    second_norm,
    second_final,
):
    left_part, right_part, gating = project_in(pair_input, first_gain, first_project, first_gate)
    left_part, right_part = (
        lax.all_to_all(left_part, ("chan", "sub"), split_axis=0, concat_axis=2, tiled=True),
        lax.all_to_all(right_part, ("chan", "sub"), split_axis=0, concat_axis=2, tiled=True),
    )
    mixture = jnp.einsum(
        "cik,cjk->cij",
        left_part,
        lax.all_gather(right_part, "dap", axis=1, tiled=True),
        preferred_element_type=jnp.float32,
    ).astype(jnp.bfloat16)
    mixture = lax.all_to_all(mixture, ("chan", "sub"), split_axis=2, concat_axis=0, tiled=True)
    middle = finish(pair_input, mixture, gating, first_norm, first_final)
    left_part, right_part, gating = project_in(middle, second_gain, second_project, second_gate)
    left_part, right_part = (
        lax.all_to_all(left_part, ("chan", "sub"), split_axis=0, concat_axis=2, tiled=True),
        lax.all_to_all(right_part, ("chan", "sub"), split_axis=0, concat_axis=2, tiled=True),
    )
    turned = lax.all_to_all(left_part, "dap", split_axis=2, concat_axis=1, tiled=True)
    mixture = jnp.einsum(
        "cki,ckj->cij",
        turned,
        lax.all_gather(right_part, "dap", axis=1, tiled=True),
        preferred_element_type=jnp.float32,
    )
    mixture = lax.all_to_all(
        mixture.astype(jnp.bfloat16), ("chan", "sub"), split_axis=2, concat_axis=0, tiled=True
    )
    return finish(middle, mixture, gating, second_norm, second_final)


def solution(mesh):
    placed = (
        P(("groups", "dap"), ("chan", "sub"), None),
        P(),
        P(),
        P(),
        P(),
        P(),
        P(),
        P(),
        P(),
        P(),
        P(),
    )
    return jax.shard_map(
        shards,
        mesh=mesh,
        in_specs=placed,
        out_specs=P(("groups", "dap"), ("chan", "sub"), None),
        check_vma=False,
    )
```

profile of v0, /device:TPU:0, one launch (start us, length us, event | category | flops | bytes accessed | tf_op | source)
XLA Modules:
  0.0 717.1 jit_solution(18188985698345366559)
XLA Ops:
  13.9 4.9 fusion.29
  26.8 4.8 copy.28
  31.6 41.2 %all_to_all.108 = bf16[128,96,96]{2,1,0:T(8,128)(2,1)S(1)} all-to-all(bf16[128,96,96]{2,1,0:T(8,128)(2,1)} %copy.28), channel_id=1, replica_groups=mesh['groups'=2,'dap'=4,'chan'=2,'sub'=2] {'chan','sub'}, dimensions={0} | all-to-all | bytes 4718592 | tf_op jit(solution)/shard_map/all_to_all | solution.py:54
  76.9 5.9 all_to_all.86
  82.9 4.8 copy.26
  87.7 53.0 %all_to_all.109 = bf16[128,96,96]{2,1,0:T(8,128)(2,1)S(1)} all-to-all(bf16[128,96,96]{2,1,0:T(8,128)(2,1)} %copy.26), channel_id=1, replica_groups=mesh['groups'=2,'dap'=4,'chan'=2,'sub'=2] {'chan','sub'}, dimensions={0} | all-to-all | bytes 4718592 | tf_op jit(solution)/shard_map/all_to_all | solution.py:53
  144.7 5.9 all_to_all.82
  150.7 100.2 %all-gather.3.cloned.1.call-done = bf16[32,384,384]{2,1,0:T(8,128)(2,1)} async-done(((bf16[32,96,384]{2,1,0:T(8,128)(2,1)}), bf16[32,384,384]{2,1,0:T(8,128)(2,1)}) %all-gather.3.cloned.1.call-update) | async-done | bytes 9437200 | tf_op jit(solution)/shard_map/all_gather | solution.py:59
  250.9 9.1 %convolution_convert_fusion.1 = bf16[32,96,384]{2,1,0:T(8,128)(2,1)} fusion(bf16[32,96,384]{2,1,0:T(8,128)(2,1)} %all_to_all.82, bf16[32,384,384]{2,1,0:T(8,128)(2,1)} %all-gather.3.cloned.1.call-done), kind=kOutput, calls=%fused_computation.61 | convolution fusion | flops 907149312 | bytes 14155776 | tf_op jit(solution)/shard_map/cik,cjk->cij/dot_general | solution.py:56
  260.0 5.0 copy.30
  265.0 4.7 all-to-all-start.2
  269.7 5.2 fusion.9
  274.9 31.7 %all-to-all-done.2 = bf16[32,96,384]{1,0,2:T(8,128)(2,1)} async-done(((bf16[32,96,384]{1,0,2:T(8,128)(2,1)}), bf16[32,96,384]{1,0,2:T(8,128)(2,1)}, u32[]{:S(2)}, u32[]{:S(2)}) %all-to-all-start.2) | async-done | bytes 2359328 | tf_op jit(solution)/shard_map/all_to_all | solution.py:62
  306.6 6.9 copy.31
  319.2 7.2 %reshape.153 = f32[128,9216]{1,0:T(8,128)} reshape(f32[4,32,96,96]{3,2,1,0:T(8,128)} %bitcast.64) | data formatting | bytes 9437184 | tf_op jit(solution)/shard_map/convert_element_type | solution.py:31
  326.4 5.9 fusion.36
  341.4 4.7 copy.37
  346.1 40.8 %all_to_all.110 = bf16[128,96,96]{2,1,0:T(8,128)(2,1)S(1)} all-to-all(bf16[128,96,96]{2,1,0:T(8,128)(2,1)} %copy.37), channel_id=1, replica_groups=mesh['groups'=2,'dap'=4,'chan'=2,'sub'=2] {'chan','sub'}, dimensions={0} | all-to-all | bytes 4718592 | tf_op jit(solution)/shard_map/all_to_all | solution.py:67
  390.9 5.9 all_to_all.99
  400.1 42.3 %all_to_all.111 = bf16[128,96,96]{2,1,0:T(8,128)(2,1)} all-to-all(bf16[128,96,96]{2,1,0:T(8,128)(2,1)} %copy.32), channel_id=1, replica_groups=mesh['groups'=2,'dap'=4,'chan'=2,'sub'=2] {'chan','sub'}, dimensions={0} | all-to-all | bytes 4718592 | tf_op jit(solution)/shard_map/all_to_all | solution.py:66
  442.4 6.6 copy.41
  449.0 159.6 %all_to_all.112 = bf16[32,96,384]{1,0,2:T(8,128)(2,1)S(1)} all-to-all(bf16[32,96,384]{1,0,2:T(8,128)(2,1)} %bitcast.71), channel_id=1, replica_groups=mesh['groups'=2,'dap'=4,'chan'=2,'sub'=2] {'dap'}, dimensions={2} | all-to-all | bytes 4718592 | tf_op jit(solution)/shard_map/all_to_all | solution.py:69
  612.6 5.0 all_to_all.95
  617.6 10.6 %all-gather.5.cloned.1.call-done = bf16[32,384,384]{2,1,0:T(8,128)(2,1)} async-done(((bf16[32,96,384]{2,1,0:T(8,128)(2,1)}), bf16[32,384,384]{2,1,0:T(8,128)(2,1)}) %all-gather.5.cloned.1.call-update) | async-done | bytes 9437200 | tf_op jit(solution)/shard_map/all_gather | solution.py:73
  628.2 7.0 convolution_convert_fusion
  635.2 5.0 copy.39
  640.2 4.9 all-to-all-start.6
  645.1 6.7 fusion.10
  651.8 30.3 %all-to-all-done.6 = bf16[32,96,384]{1,0,2:T(8,128)(2,1)} async-done(((bf16[32,96,384]{1,0,2:T(8,128)(2,1)}), bf16[32,96,384]{1,0,2:T(8,128)(2,1)}, u32[]{:S(2)}, u32[]{:S(2)}) %all-to-all-start.6) | async-done | bytes 2359328 | tf_op jit(solution)/shard_map/all_to_all | solution.py:76
  682.1 6.9 copy.40
  694.7 7.2 %reshape.154 = f32[128,9216]{1,0:T(8,128)} reshape(f32[4,32,96,96]{3,2,1,0:T(8,128)} %bitcast.65) | data formatting | bytes 9437184 | tf_op jit(solution)/shard_map/convert_element_type | solution.py:31
  701.9 8.0 %fusion.7 = bf16[9216,128]{1,0:T(8,128)(2,1)} fusion(f32[9216,128]{1,0:T(8,128)} %copy-done.4, f32[9216,128]{1,0:T(8,128)} %fusion.10, bf16[128,128]{1,0:T(8,128)(2,1)S(1)} %copy-done.9, f32[128,9216]{1,0:T(8,128)} %reshape.154, f32[128]{0:T(128)S(1)} %copy-done.13, f32[9216]{0:T(1024)S(1)} %rsqrt.47, f32[9216]{0:T(1024)S(1)} %div.63), kind=kOutput, calls=%fused_computation.13 | convolution fusion | flops 310247424 | bytes 16622080 | tf_op jit(solution)/shard_map/cx,cd->xd/dot_general | solution.py:33
  (66 shorter events, 55.0 us)
Async XLA Ops:
  6.5 13.7 %copy-start = (bf16[128,512]{1,0:T(8,128)(2,1)S(1)}, bf16[128,512]{1,0:T(8,128)(2,1)}, u32[]{:S(2)}) copy-start(bf16[128,512]{1,0:T(8,128)(2,1)} %param.13) | copy-start | bytes 393220
  6.5 7.3 %copy-start.5 = (bf16[96,96,128]{2,1,0:T(8,128)(2,1)S(1)}, bf16[96,96,128]{2,1,0:T(8,128)(2,1)}, u32[]{:S(2)}) copy-start(bf16[96,96,128]{2,1,0:T(8,128)(2,1)} %param.11) | copy-start | bytes 7077892
  6.5 7.3 %copy-start.12 = (f32[128]{0:T(128)S(1)}, f32[128]{0:T(128)}, u32[]{:S(2)}) copy-start(f32[128]{0:T(128)} %param.12) | copy-start | bytes 1540
  6.5 244.4 %all-gather.3.cloned.1.call-start = ((), (), s32[]{:S(2)}) async-start(), calls=%async_computation.7 | async-start | bytes 11796480 | tf_op jit(solution)/shard_map/all_gather | solution.py:59
  18.9 1.4 copy-start.6
  260.0 9.7 %copy-start.14 = (bf16[128,128]{1,0:T(8,128)(2,1)S(1)}, bf16[128,128]{1,0:T(8,128)(2,1)}, u32[]{:S(2)}) copy-start(bf16[128,128]{1,0:T(8,128)(2,1)} %param.14) | copy-start | bytes 98308
  265.0 41.6 %all-to-all-start.2 = ((bf16[32,96,384]{1,0,2:T(8,128)(2,1)}), bf16[32,96,384]{1,0,2:T(8,128)(2,1)}, u32[]{:S(2)}, u32[]{:S(2)}) async-start(bf16[32,96,384]{1,0,2:T(8,128)(2,1)} %copy.30), calls=%async_computation.2 | async-start | bytes 6291456 | tf_op jit(solution)/shard_map/all_to_all | solution.py:62
  269.7 358.5 %all-gather.5.cloned.1.call-start = ((), (), s32[]{:S(2)}) async-start(), calls=%async_computation.8 | async-start | bytes 11796480 | tf_op jit(solution)/shard_map/all_gather | solution.py:73
  313.5 4.6 copy-start.2
  319.2 7.2 %copy-start.8 = (bf16[128,128]{1,0:T(8,128)(2,1)S(1)}, bf16[128,128]{1,0:T(8,128)(2,1)}, u32[]{:S(2)}) copy-start(bf16[128,128]{1,0:T(8,128)(2,1)} %param.16) | copy-start | bytes 98308
  319.2 7.2 %copy-start.11 = (f32[128]{0:T(128)S(1)}, f32[128]{0:T(128)}, u32[]{:S(2)}) copy-start(f32[128]{0:T(128)} %param.15) | copy-start | bytes 1540
  332.3 5.5 copy-start.4
  332.4 2.8 copy-start.7
  332.4 2.8 copy-start.10
  635.2 9.9 %copy-start.15 = (bf16[128,128]{1,0:T(8,128)(2,1)S(1)}, bf16[128,128]{1,0:T(8,128)(2,1)}, u32[]{:S(2)}) copy-start(bf16[128,128]{1,0:T(8,128)(2,1)} %param.19) | copy-start | bytes 98308
  640.2 41.8 %all-to-all-start.6 = ((bf16[32,96,384]{1,0,2:T(8,128)(2,1)}), bf16[32,96,384]{1,0,2:T(8,128)(2,1)}, u32[]{:S(2)}, u32[]{:S(2)}) async-start(bf16[32,96,384]{1,0,2:T(8,128)(2,1)} %copy.39), calls=%async_computation.6 | async-start | bytes 6291456 | tf_op jit(solution)/shard_map/all_to_all | solution.py:76
  689.0 4.6 copy-start.3
  694.6 7.2 %copy-start.9 = (bf16[128,128]{1,0:T(8,128)(2,1)S(1)}, bf16[128,128]{1,0:T(8,128)(2,1)}, u32[]{:S(2)}) copy-start(bf16[128,128]{1,0:T(8,128)(2,1)} %param.21) | copy-start | bytes 98308
  694.7 7.2 %copy-start.13 = (f32[128]{0:T(128)S(1)}, f32[128]{0:T(128)}, u32[]{:S(2)}) copy-start(f32[128]{0:T(128)} %param.20) | copy-start | bytes 1540
  694.7 15.2 %copy-start.1 = (bf16[128,512]{1,0:T(8,128)(2,1)S(1)}, bf16[128,512]{1,0:T(8,128)(2,1)}, u32[]{:S(2)}) copy-start(bf16[128,512]{1,0:T(8,128)(2,1)} %param.13) | copy-start | bytes 393220
Sparse Core Ops, SparseCore 0:
  83.0 167.8 all-gather.2
  397.0 231.1 all-gather.4
where the time goes:
time: 727 us; the launch traced here: 717 us
  blocking collectives  337 us (46%)
  waiting for transfers between devices  173 us (24%)
  local copies, waits for them, and re-layouts  106 us (15%)
  matrix products  47 us (6%)
  other arithmetic  30.8 us (4%)
  between operations  14.1 us (2%)
  starting transfers between devices  9.58 us (1%)
    all_to_all x1, blocking collectives, shards(): lax.all_to_all(left_part, 'dap', split_axis=2, concat_axis=1, tiled=True)  160 us
    all_gather x2, waiting for transfers between devices, shards(): lax.all_gather(right_part, 'dap', axis=1, tiled=True)  111 us
    all_to_all x2, blocking collectives, shards(): lax.all_to_all(left_part, ('chan', 'sub'), split_axis=0, concat_axis=2, t...  95.4 us
    all_to_all x2, blocking collectives, shards(): lax.all_to_all(right_part, ('chan', 'sub'), split_axis=0, concat_axis=2,...  82 us
    all_to_all x1, waiting for transfers between devices, shards(): lax.all_to_all(mixture, ('chan', 'sub'), split_axis=2, concat_axis=0, til...  31.7 us
    all_to_all x1, waiting for transfers between devices, shards(): lax.all_to_all(mixture.astype(jnp.bfloat16), ('chan', 'sub'), split_axis=...  30.3 us
    convert_element_type x4, local copies, waits for them, and re-layouts, finish(): flattened = mixture.reshape(features, -1).astype(jnp.float32)  28.1 us
    all_to_all x4, local copies, waits for them, and re-layouts, shards(): lax.all_to_all(right_part, ('chan', 'sub'), split_axis=0, concat_axis=2,...  20 us
  transfers between devices with their start and end apart: 4, of which 4 were waited for; matrix products, arithmetic and copies ran while one was open for 5% of the time, Pallas kernels for 0%

commit v1 on v0

--- a/solution.py
+++ b/solution.py
@@ -1,9 +1,22 @@
+import functools
 import jax
 import jax.numpy as jnp
 from jax import lax
 from jax.sharding import PartitionSpec as P
+from jax.lax import all_to_all, axis_size
 
 epsilon = 1e-05
+
+
+def process_lots_all_for(xin, device_axis):
+    found_now = axis_size(device_axis)
+    passed = jnp.split(xin, found_now, axis=2)
+    state_now = jnp.stack(passed)
+    response = all_to_all(state_now, device_axis, 0, 0)
+    return jnp.concatenate(response, axis=1)
+
+
+use_column_over_axis = functools.partial(process_lots_all_for, device_axis="dap")
 
 
 def layer_norm(values, norm_gain, reduce_axis):
@@ -66,7 +79,7 @@
         lax.all_to_all(left_part, ("chan", "sub"), split_axis=0, concat_axis=2, tiled=True),
         lax.all_to_all(right_part, ("chan", "sub"), split_axis=0, concat_axis=2, tiled=True),
     )
-    turned = lax.all_to_all(left_part, "dap", split_axis=2, concat_axis=1, tiled=True)
+    turned = use_column_over_axis(left_part)
     mixture = jnp.einsum(
         "cki,ckj->cij",
         turned,

time: 727 us -> 727 us (level)
    reshape x0 -> x2, local copies, waits for them, and re-layouts: none -> 11.4 us  [process_lots_all_for(): return jnp.concatenate(response, axis=1)]
    all_to_all x2 -> x0, local copies, waits for them, and re-layouts: 9 us -> none  [shards(): lax.all_to_all(left_part, 'dap', split_axis=2, concat_axis=1, tiled=True)]
    all_to_all x3 -> x4, local copies, waits for them, and re-layouts: 16.5 us -> 19 us  [shards(): lax.all_to_all(left_part, ('chan', 'sub'), split_axis=0, concat_axis=2, t...]
  transfers between devices with their start and end apart: 4 -> 4, of which waited for: 4 -> 4; matrix products, arithmetic and copies ran while one was open for 5% -> 6% of each run, Pallas kernels for 0% -> 0%
where the time goes in v1:
time: 727 us; the launch traced here: 717 us
  blocking collectives  335 us (46%)
  waiting for transfers between devices  168 us (23%)
  local copies, waits for them, and re-layouts  112 us (15%)
  matrix products  47 us (6%)
  other arithmetic  31.7 us (4%)
  between operations  14.1 us (2%)
  starting transfers between devices  9.61 us (1%)
    all_to_all x1, blocking collectives, process_lots_all_for(): response = all_to_all(state_now, device_axis, 0, 0)  159 us
    all_gather x2, waiting for transfers between devices, shards(): lax.all_gather(right_part, 'dap', axis=1, tiled=True)  106 us
    all_to_all x2, blocking collectives, shards(): lax.all_to_all(left_part, ('chan', 'sub'), split_axis=0, concat_axis=2, t...  93.7 us
    all_to_all x2, blocking collectives, shards(): lax.all_to_all(right_part, ('chan', 'sub'), split_axis=0, concat_axis=2,...  82 us
    all_to_all x1, waiting for transfers between devices, shards(): lax.all_to_all(mixture, ('chan', 'sub'), split_axis=2, concat_axis=0, til...  31.7 us
    all_to_all x1, waiting for transfers between devices, shards(): lax.all_to_all(mixture.astype(jnp.bfloat16), ('chan', 'sub'), split_axis=...  30.3 us
    convert_element_type x4, local copies, waits for them, and re-layouts, finish(): flattened = mixture.reshape(features, -1).astype(jnp.float32)  28.1 us
    all_to_all x4, local copies, waits for them, and re-layouts, shards(): lax.all_to_all(right_part, ('chan', 'sub'), split_axis=0, concat_axis=2,...  20 us
  transfers between devices with their start and end apart: 4, of which 4 were waited for; matrix products, arithmetic and copies ran while one was open for 6% of the time, Pallas kernels for 0%

profile of v1, /device:TPU:0, one launch (start us, length us, event | category | flops | bytes accessed | tf_op | source)
XLA Modules:
  0.0 717.3 jit_solution(16066359954950217453)
XLA Ops:
  13.9 4.9 fusion.29
  26.8 4.9 copy.42
  31.6 41.2 %all_to_all.95 = bf16[128,96,96]{2,1,0:T(8,128)(2,1)S(1)} all-to-all(bf16[128,96,96]{2,1,0:T(8,128)(2,1)} %copy.42), channel_id=1, replica_groups=mesh['groups'=2,'dap'=4,'chan'=2,'sub'=2] {'chan','sub'}, dimensions={0} | all-to-all | bytes 4718592 | tf_op jit(solution)/shard_map/all_to_all | solution.py:67
  77.0 5.9 all_to_all.76
  82.9 4.8 copy.40
  87.8 53.0 %all_to_all.96 = bf16[128,96,96]{2,1,0:T(8,128)(2,1)S(1)} all-to-all(bf16[128,96,96]{2,1,0:T(8,128)(2,1)} %copy.40), channel_id=1, replica_groups=mesh['groups'=2,'dap'=4,'chan'=2,'sub'=2] {'chan','sub'}, dimensions={0} | all-to-all | bytes 4718592 | tf_op jit(solution)/shard_map/all_to_all | solution.py:66
  144.8 5.9 all_to_all.72
  150.8 100.2 %all-gather.3.cloned.1.call-done = bf16[32,384,384]{2,1,0:T(8,128)(2,1)} async-done(((bf16[32,96,384]{2,1,0:T(8,128)(2,1)}), bf16[32,384,384]{2,1,0:T(8,128)(2,1)}) %all-gather.3.cloned.1.call-update) | async-done | bytes 9437200 | tf_op jit(solution)/shard_map/all_gather | solution.py:72
  251.0 9.1 %convolution_convert_fusion.1 = bf16[32,96,384]{2,1,0:T(8,128)(2,1)} fusion(bf16[32,96,384]{2,1,0:T(8,128)(2,1)} %all_to_all.72, bf16[32,384,384]{2,1,0:T(8,128)(2,1)} %all-gather.3.cloned.1.call-done), kind=kOutput, calls=%fused_computation.61 | convolution fusion | flops 907149312 | bytes 14155776 | tf_op jit(solution)/shard_map/cik,cjk->cij/dot_general | solution.py:69
  260.0 5.0 copy.44
  269.8 5.2 fusion.9
  275.0 31.7 %all-to-all-done.2 = bf16[32,96,384]{1,0,2:T(8,128)(2,1)} async-done(((bf16[32,96,384]{1,0,2:T(8,128)(2,1)}), bf16[32,96,384]{1,0,2:T(8,128)(2,1)}, u32[]{:S(2)}, u32[]{:S(2)}) %all-to-all-start.2) | async-done | bytes 2359328 | tf_op jit(solution)/shard_map/all_to_all | solution.py:75
  306.7 6.9 copy.45
  319.3 7.2 %reshape.161 = f32[128,9216]{1,0:T(8,128)} reshape(f32[4,32,96,96]{3,2,1,0:T(8,128)} %bitcast.67) | data formatting | bytes 9437184 | tf_op jit(solution)/shard_map/convert_element_type | solution.py:44
  326.5 5.9 fusion.36
  341.4 4.8 copy.49
  346.3 40.8 %all_to_all.97 = bf16[128,96,96]{2,1,0:T(8,128)(2,1)S(1)} all-to-all(bf16[128,96,96]{2,1,0:T(8,128)(2,1)} %copy.49), channel_id=1, replica_groups=mesh['groups'=2,'dap'=4,'chan'=2,'sub'=2] {'chan','sub'}, dimensions={0} | all-to-all | bytes 4718592 | tf_op jit(solution)/shard_map/all_to_all | solution.py:80
  391.1 5.9 all_to_all.86
  400.2 40.7 %all_to_all.98 = bf16[128,96,96]{2,1,0:T(8,128)(2,1)S(1)} all-to-all(bf16[128,96,96]{2,1,0:T(8,128)(2,1)} %copy.46), channel_id=1, replica_groups=mesh['groups'=2,'dap'=4,'chan'=2,'sub'=2] {'chan','sub'}, dimensions={0} | all-to-all | bytes 4718592 | tf_op jit(solution)/shard_map/all_to_all | solution.py:79
  445.0 5.0 all_to_all.81
  451.7 159.2 %all_to_all.99 = bf16[4,32,96,96]{3,2,1,0:T(8,128)(2,1)} all-to-all(bf16[4,32,96,96]{3,2,1,0:T(8,128)(2,1)S(1)} %pad_maximum_fusion), channel_id=1, replica_groups=mesh['groups'=2,'dap'=4,'chan'=2,'sub'=2] {'dap'}, dimensions={0} | all-to-all | bytes 4718592 | tf_op jit(solution)/shard_map/all_to_all | solution.py:15
  610.9 6.5 copy.48
  617.4 5.0 reshape.157
  622.3 6.0 all-gather.5.cloned.1.call-done
  628.4 7.0 convolution_convert_fusion
  635.4 5.0 copy.51
  640.4 4.9 all-to-all-start.6
  645.3 6.7 fusion.10
  652.0 30.3 %all-to-all-done.6 = bf16[32,96,384]{1,0,2:T(8,128)(2,1)} async-done(((bf16[32,96,384]{1,0,2:T(8,128)(2,1)}), bf16[32,96,384]{1,0,2:T(8,128)(2,1)}, u32[]{:S(2)}, u32[]{:S(2)}) %all-to-all-start.6) | async-done | bytes 2359328 | tf_op jit(solution)/shard_map/all_to_all | solution.py:89
  682.3 6.9 copy.52
  694.9 7.2 %reshape.162 = f32[128,9216]{1,0:T(8,128)} reshape(f32[4,32,96,96]{3,2,1,0:T(8,128)} %bitcast.68) | data formatting | bytes 9437184 | tf_op jit(solution)/shard_map/convert_element_type | solution.py:44
  702.0 8.0 %fusion.7 = bf16[9216,128]{1,0:T(8,128)(2,1)} fusion(f32[9216,128]{1,0:T(8,128)} %copy-done.4, f32[9216,128]{1,0:T(8,128)} %fusion.10, bf16[128,128]{1,0:T(8,128)(2,1)S(1)} %copy-done.9, f32[128,9216]{1,0:T(8,128)} %reshape.162, f32[128]{0:T(128)S(1)} %copy-done.13, f32[9216]{0:T(1024)S(1)} %rsqrt.47, f32[9216]{0:T(1024)S(1)} %div.63), kind=kOutput, calls=%fused_computation.13 | convolution fusion | flops 310247424 | bytes 16622080 | tf_op jit(solution)/shard_map/cx,cd->xd/dot_general | solution.py:46
  (69 shorter events, 61.4 us)
Async XLA Ops:
  6.5 13.7 %copy-start = (bf16[128,512]{1,0:T(8,128)(2,1)S(1)}, bf16[128,512]{1,0:T(8,128)(2,1)}, u32[]{:S(2)}) copy-start(bf16[128,512]{1,0:T(8,128)(2,1)} %param.13) | copy-start | bytes 393220
  6.5 7.3 %copy-start.5 = (bf16[96,96,128]{2,1,0:T(8,128)(2,1)S(1)}, bf16[96,96,128]{2,1,0:T(8,128)(2,1)}, u32[]{:S(2)}) copy-start(bf16[96,96,128]{2,1,0:T(8,128)(2,1)} %param.11) | copy-start | bytes 7077892
  6.5 7.3 %copy-start.12 = (f32[128]{0:T(128)S(1)}, f32[128]{0:T(128)}, u32[]{:S(2)}) copy-start(f32[128]{0:T(128)} %param.12) | copy-start | bytes 1540
  6.5 244.4 %all-gather.3.cloned.1.call-start = ((), (), s32[]{:S(2)}) async-start(), calls=%async_computation.7 | async-start | bytes 11796480 | tf_op jit(solution)/shard_map/all_gather | solution.py:72
  18.9 1.4 copy-start.6
  260.0 9.8 %copy-start.14 = (bf16[128,128]{1,0:T(8,128)(2,1)S(1)}, bf16[128,128]{1,0:T(8,128)(2,1)}, u32[]{:S(2)}) copy-start(bf16[128,128]{1,0:T(8,128)(2,1)} %param.14) | copy-start | bytes 98308
  265.1 41.6 %all-to-all-start.2 = ((bf16[32,96,384]{1,0,2:T(8,128)(2,1)}), bf16[32,96,384]{1,0,2:T(8,128)(2,1)}, u32[]{:S(2)}, u32[]{:S(2)}) async-start(bf16[32,96,384]{1,0,2:T(8,128)(2,1)} %copy.44), calls=%async_computation.2 | async-start | bytes 6291456 | tf_op jit(solution)/shard_map/all_to_all | solution.py:75
  269.7 358.6 %all-gather.5.cloned.1.call-start = ((), (), s32[]{:S(2)}) async-start(), calls=%async_computation.8 | async-start | bytes 11796480 | tf_op jit(solution)/shard_map/all_gather | solution.py:86
  313.6 4.6 copy-start.2
  319.3 7.2 %copy-start.8 = (bf16[128,128]{1,0:T(8,128)(2,1)S(1)}, bf16[128,128]{1,0:T(8,128)(2,1)}, u32[]{:S(2)}) copy-start(bf16[128,128]{1,0:T(8,128)(2,1)} %param.16) | copy-start | bytes 98308
  319.3 7.2 %copy-start.11 = (f32[128]{0:T(128)S(1)}, f32[128]{0:T(128)}, u32[]{:S(2)}) copy-start(f32[128]{0:T(128)} %param.15) | copy-start | bytes 1540
  332.4 5.5 copy-start.4
  332.4 2.8 copy-start.7
  332.4 2.8 copy-start.10
  635.4 10.0 %copy-start.15 = (bf16[128,128]{1,0:T(8,128)(2,1)S(1)}, bf16[128,128]{1,0:T(8,128)(2,1)}, u32[]{:S(2)}) copy-start(bf16[128,128]{1,0:T(8,128)(2,1)} %param.19) | copy-start | bytes 98308
  640.4 41.9 %all-to-all-start.6 = ((bf16[32,96,384]{1,0,2:T(8,128)(2,1)}), bf16[32,96,384]{1,0,2:T(8,128)(2,1)}, u32[]{:S(2)}, u32[]{:S(2)}) async-start(bf16[32,96,384]{1,0,2:T(8,128)(2,1)} %copy.51), calls=%async_computation.6 | async-start | bytes 6291456 | tf_op jit(solution)/shard_map/all_to_all | solution.py:89
  689.1 4.6 copy-start.3
  694.8 7.2 %copy-start.9 = (bf16[128,128]{1,0:T(8,128)(2,1)S(1)}, bf16[128,128]{1,0:T(8,128)(2,1)}, u32[]{:S(2)}) copy-start(bf16[128,128]{1,0:T(8,128)(2,1)} %param.21) | copy-start | bytes 98308
  694.8 7.2 %copy-start.13 = (f32[128]{0:T(128)S(1)}, f32[128]{0:T(128)}, u32[]{:S(2)}) copy-start(f32[128]{0:T(128)} %param.20) | copy-start | bytes 1540
  694.8 15.2 %copy-start.1 = (bf16[128,512]{1,0:T(8,128)(2,1)S(1)}, bf16[128,512]{1,0:T(8,128)(2,1)}, u32[]{:S(2)}) copy-start(bf16[128,512]{1,0:T(8,128)(2,1)} %param.13) | copy-start | bytes 393220
Sparse Core Ops, SparseCore 0:
  83.0 167.8 all-gather.2
  397.2 231.1 all-gather.4
